TPU v7x, 32 devices: a whole 2x2x4 slice. The times are simulated.
32 devices in a mesh: space: 16 (over z, x, core), trial: 2 (over y).
Axes of the slice: x: 2, y: 2, z: 4, core: 2. Of those that a mesh axis runs over, the one named last changes fastest.
Arguments:
- trial_x: bfloat16 [4, 4096, 1024], P('trial', 'space')
- h_panel: bfloat16 [4096, 640], P('space')
- s_panel: bfloat16 [4096, 640], P('space')
- pattern: int32 [64, 10], P('space'), may hold values from 0 to 63, as said below
Outputs:
- theta: float32 [4], P('trial')
- new_dirs: bfloat16 [4, 4096, 1024], P('trial', 'space')
- mean_sq: float32 [4], P('trial')
Inputs may be any that keep to these rules, and one draw needn't show every extreme that they name: pattern[a, 0] is a; the entries of a row are distinct atoms of a's own spatial domain or of the two domains beside it (cyclically), the domain of atom a being a // 4.
All inputs are finite; a program needn't handle non-finite values.
Results may differ from a plain program's by a relative error of at most 0.0006.
Values may be sent and summed in bfloat16 or wider, within the bound.
A program may use at most 128 MiB of HBM per device.

v0:
```python
import jax
import jax.numpy as jnp
from jax import lax
from jax.sharding import PartitionSpec as P


def padded(x, sides, width):
    for axis, dim in sides:
        peers, length = (lax.axis_size(axis), x.shape[dim])
        up = [(i, (i + 1) % peers) for i in range(peers)]
        down = [(j, i) for i, j in up]
        last = lax.slice_in_dim(x, length - width, length, axis=dim)
        first = lax.slice_in_dim(x, 0, width, axis=dim)
        before = lax.ppermute(last, axis, up)
        after = lax.ppermute(first, axis, down)
        x = jnp.concatenate([before, x, after], axis=dim)
    return x


def neighbours(values, width):
    return padded(values, (("space", 1),), width)


def apply_tiles(h_panel, s_panel, links, extended, block):
    count, ext_rows, width = extended.shape
    atom_dev, slots = links.shape
    blocks = extended.reshape(count, ext_rows // block, block, width)
    picked = blocks[:, links]
    h_tiles = h_panel.reshape(atom_dev, block, slots, block)
    s_tiles = s_panel.reshape(atom_dev, block, slots, block)
    h_image = jnp.einsum("apbq,kabqw->kapw", h_tiles, picked, preferred_element_type=jnp.float32)
    s_image = jnp.einsum("apbq,kabqw->kapw", s_tiles, picked, preferred_element_type=jnp.float32)
    return (h_image.reshape(count, -1), s_image.reshape(count, -1))


def row_reduce(section, values):
    if section == "ritz":
        return lax.psum(values, "space")
    if section == "project":
        return lax.psum(values, "space")
    return lax.psum(values, "space")


def solve_coeffs(gram, correlation):
    factor = jnp.linalg.cholesky(gram)
    return jax.scipy.linalg.cho_solve((factor, True), correlation)


def finish(x_every, mine_shape, flat_h, flat_s, reducer, total):
    flat_all = x_every.reshape(x_every.shape[0], -1)
    gram_part = jnp.dot(flat_all, flat_all.T, preferred_element_type=jnp.float32)
    wide_all = flat_all.astype(jnp.float32)
    cross = jnp.sum(flat_s * flat_h, axis=1)
    weight = jnp.sum(flat_s * flat_s, axis=1)
    cross, weight, gram = reducer("ritz", (cross, weight, gram_part))
    theta = cross / (weight + 1e-06)
    flat_r = flat_h - theta[:, None] * flat_s
    correlation = reducer("project", jnp.dot(wide_all, flat_r.T, precision=lax.Precision.HIGHEST))
    coeffs = solve_coeffs(gram, correlation)
    normal_part = flat_r - jnp.dot(coeffs.T, wide_all, precision=lax.Precision.HIGHEST)
    mean_sq = reducer("norm", jnp.sum(normal_part * normal_part, axis=1)) / total
    scaled = normal_part * lax.rsqrt(mean_sq + 1e-06)[:, None]
    return (theta, scaled.astype(jnp.bfloat16).reshape(mine_shape), mean_sq)


def on_device(trial_x, h_panel, s_panel, pattern):
    atom_dev = pattern.shape[0]
    block = h_panel.shape[0] // atom_dev
    domains = lax.axis_size("space")
    atoms = atom_dev * domains
    links = jnp.mod(pattern - lax.axis_index("space") * atom_dev + atom_dev, atoms)
    total = float(atoms * block * trial_x.shape[2])
    x_every = lax.all_gather(trial_x, "trial", axis=0, tiled=True)
    flat_h, flat_s = apply_tiles(
        h_panel, s_panel, links, neighbours(trial_x, atom_dev * block), block
    )
    theta, normed, mean_sq = finish(x_every, trial_x.shape, flat_h, flat_s, row_reduce, total)
    return (theta, normed, mean_sq)


def solution(mesh):
    in_specs = (P("trial", "space", None), P("space", None), P("space", None), P("space", None))
    out_specs = (P("trial"), P("trial", "space", None), P("trial"))
    return jax.shard_map(
        on_device, mesh=mesh, in_specs=in_specs, out_specs=out_specs, check_vma=False
    )
```

profile of v0, /device:TPU:0, one launch (start us, length us, event | category | flops | bytes accessed | tf_op | source)
XLA Modules:
  0.0 193.6 jit_solution(5035406191406211222)
XLA Ops:
  7.2 0.0 copy-start.8
  7.2 0.0 all-gather.2.cloned.1.call-start
  7.2 0.5 collective-permute-start
  7.7 5.0 %collective-permute-start.1 = (bf16[2,256,1024]{2,1,0:T(8,128)(2,1)}, bf16[2,256,1024]{2,1,0:T(8,128)(2,1)}, u32[]{:S(2)}, u32[]{:S(2)}) collective-permute-start(bf16[2,256,1024]{2,1,0:T(8,128)(2,1)} %param.4), channel_id=1, source_target_pairs={{2,0},{4,2},{6,4},{8,6},{10,8},{12,10},{14,12},{16,14},{18,16},{20... | collective-permute-start | bytes 3145736 | tf_op jit(solution)/shard_map/ppermute | solution.py:15
  12.8 0.0 all-gather.2.cloned.1.call-update
  12.8 0.7 compare_select_fusion
  13.5 0.1 reshape.56
  13.6 2.4 %reshape.70 = bf16[4,64,10,64]{3,2,1,0:T(8,128)(2,1)} reshape(bf16[256,640]{1,0:T(8,128)(2,1)} %param.5) | data formatting | bytes 655360 | tf_op jit(solution)/shard_map/reshape | solution.py:29
  16.0 0.0 copy-done.8
  16.0 1.6 reshape.69
  17.6 7.9 %collective-permute-done = bf16[2,256,1024]{2,1,0:T(8,128)(2,1)S(1)} collective-permute-done((bf16[2,256,1024]{2,1,0:T(8,128)(2,1)}, bf16[2,256,1024]{2,1,0:T(8,128)(2,1)S(1)}, u32[]{:S(2)}, u32[]{:S(2)}) %collective-permute-start) | collective-permute-done | bytes 1048608 | tf_op jit(solution)/shard_map/ppermute | solution.py:14
  25.5 0.0 copy-start.7
  25.5 1.0 copy-done.7
  26.5 0.0 collective-permute-done.1
  26.5 2.0 %pad_maximum_fusion = bf16[2,768,1024]{2,1,0:T(8,128)(2,1)S(1)} fusion(bf16[2,256,1024]{2,1,0:T(8,128)(2,1)} %collective-permute-done.1, bf16[2,256,1024]{2,1,0:T(8,128)(2,1)} %param.4, bf16[2,256,1024]{2,1,0:T(8,128)(2,1)} %copy-done.7), kind=kLoop, calls=%fused_computation.6 | loop fusion | flops 9437184 | bytes 6291456 | tf_op jit(solution)/shard_map/concatenate | solution.py:16
  28.5 5.8 %gather_fusion = bf16[40,2,64,1024]{3,2,1,0:T(8,128)(2,1)} fusion(bf16[2,12,64,1024]{3,2,1,0:T(8,128)(2,1)S(1)} %bitcast.54, s32[1024]{0:T(1024)S(1)} %pad_clamp_fusion), kind=kCustom, calls=%fused_computation | custom fusion | bytes 20971680 | tf_op jit(solution)/shard_map/gather | solution.py:28
  34.2 0.0 copy-start
  34.2 0.0 copy-start.6
  34.2 6.5 %fusion.6 = f32[2,4,64,1024]{3,2,0,1:T(8,128)S(1)} fusion(bf16[2,4,10,64,1024]{4,3,0,2,1:T(8,128)(2,1)} %bitcast.55, bf16[4,64,10,64,1]{3,2,1,0,4:T(8,128)(2,1)} %bitcast.68), kind=kOutput, calls=%fused_computation.14 | convolution fusion | flops 671088640 | bytes 12910592 | tf_op jit(solution)/shard_map/apbq,kabqw->kapw/dot_general | solution.py:31
  40.7 0.8 copy-done
  41.5 0.2 copy-done.6
  41.7 3.5 %multiply_reduce_fusion.1 = (f32[2]{0:T(128)S(1)}, f32[2]{0:T(128)S(1)}, f32[2,4,64,1024]{3,2,0,1:T(8,128)}) fusion(f32[2,4,64,1024]{3,2,0,1:T(8,128)S(1)} %fusion.6, bf16[2,4,10,64,1024]{4,3,0,2,1:T(8,128)(2,1)S(1)} %bitcast.56, bf16[4,64,10,64,1]{3,2,1,0,4:T(8,128)(2,1)S(1)} %bitcast.67), kind=kOutput, calls=%fused_computation.10 | convolution fusion | flops 673185792 | bytes 15007760 | tf_op jit(solution)/shard_map/apbq,kabqw->kapw/dot_general | solution.py:32
  45.2 39.5 %all-reduce.1 = (f32[2]{0:T(128)S(1)}, f32[2]{0:T(128)S(1)}) all-reduce(f32[2]{0:T(128)S(1)} %get-tuple-element.4, f32[2]{0:T(128)S(1)} %get-tuple-element.3), channel_id=1, replica_groups=mesh['space'=16,'trial'=2] {'space'}, use_global_device_ids=true, to_apply=%region_1.2 | all-reduce | flops 4 | bytes 32 | tf_op jit(solution)/shard_map/psum | solution.py:38
  84.8 0.0 copy-start.1
  84.8 1.4 copy.32
  86.2 0.9 copy-done.1
  87.1 0.1 copy.33
  87.3 0.0 copy-start.9
  87.3 0.5 multiply_subtract_fusion
  87.8 0.1 copy.39
  87.9 2.9 %copy.56 = f32[1,2,256,1024]{3,1,2,0:T(2,128)} copy(f32[1,2,256,1024]{3,2,1,0:T(8,128)S(1)} %bitcast.59) | data formatting | bytes 4194304
  90.9 1.6 copy.55
  92.5 0.0 all-gather.2.cloned.1.call-done
  92.5 0.0 copy-start.5
  92.5 3.4 %copy.57 = bf16[1,4,256,1024]{3,1,2,0:T(4,128)(2,1)S(1)} copy(bf16[1,4,256,1024]{3,2,1,0:T(8,128)(2,1)} %bitcast.61) | data formatting | bytes 4194304
  95.9 0.0 copy-start.4
  95.9 1.3 copy-done.4
  97.2 0.0 copy-done.5
  97.2 0.0 copy-start.3
  97.2 9.2 %convolution_bitcast_fusion = f32[4,2]{0,1:T(2,128)S(1)} fusion(f32[2,262144]{1,0:T(2,128)S(1)} %bitcast.66, bf16[4,262144]{1,0:T(4,128)(2,1)S(1)} %bitcast.63), kind=kOutput, calls=%fused_computation.17 | convolution fusion | flops 25165824 | bytes 4194336 | tf_op jit(solution)/shard_map/dot_general | solution.py:58
  106.4 0.0 copy-done.3
  106.4 0.0 copy-start.2
  106.4 3.5 %fusion.12 = f32[4,4]{0,1:T(4,128)S(1)} fusion(bf16[4,256,1024]{2,1,0:T(8,128)(2,1)S(1)} %copy-done.3), kind=kOutput, calls=%fused_computation.16 | convolution fusion | flops 8388608 | bytes 2097216 | tf_op jit(solution)/shard_map/dot_general | solution.py:51
  109.9 0.0 copy-done.2
  109.9 2.9 %copy.54 = f32[1,2,256,1024]{3,1,2,0:T(2,128)} copy(f32[1,2,256,1024]{3,2,1,0:T(8,128)S(1)} %bitcast.57) | data formatting | bytes 4194304
  112.9 29.5 %all-reduce = (f32[4,2]{0,1:T(2,128)S(1)}, f32[4,4]{0,1:T(4,128)S(1)}) all-reduce(f32[4,2]{0,1:T(2,128)S(1)} %convolution_bitcast_fusion, f32[4,4]{0,1:T(4,128)S(1)} %fusion.12), channel_id=1, replica_groups=mesh['space'=16,'trial'=2] {'space'}, use_global_device_ids=true, to_apply=%region_7.8 | all-reduce | flops 24 | bytes 192 | tf_op jit(solution)/shard_map/psum | solution.py:40
  142.3 0.1 copy.37
  142.4 0.4 cholesky.16
  142.8 0.6 compare_reduce_fusion
  143.5 0.6 fusion.17
  144.1 0.3 custom-call.10
  144.5 0.1 fusion.19
  144.6 0.1 fusion.21
  144.7 0.0 copy-done.9
  144.7 8.7 %multiply_reduce_fusion = (f32[2]{0:T(128)S(1)}, f32[2,262144]{1,0:T(2,128)}) fusion(f32[4,2]{0,1:T(2,128)S(1)} %fusion.21, bf16[4,262144]{1,0:T(4,128)(2,1)} %bitcast.64, f32[2,262144]{1,0:T(2,128)} %bitcast.65, f32[2,262144]{1,0:T(2,128)S(1)} %bitcast.62, f32[2]{0:T(128)S(1)} %add_divide_fusion), kind=kOutput, calls=%fused_computation.8 | convolution fusion | flops 27787262 | bytes 8388656 | tf_op jit(solution)/shard_map/dot_general | solution.py:60
  153.4 29.5 %psum.39 = f32[2]{0:T(128)S(1)} all-reduce(f32[2]{0:T(128)S(1)} %get-tuple-element.12), channel_id=1, replica_groups=mesh['space'=16,'trial'=2] {'space'}, use_global_device_ids=true, to_apply=%region_9.10 | all-reduce | flops 2 | bytes 16 | tf_op jit(solution)/shard_map/psum | solution.py:41
  182.9 0.5 add_rsqrt_fusion
  183.4 2.1 %multiply_convert_fusion = bf16[2,262144]{1,0:T(2,128)(2,1)S(1)} fusion(f32[2,262144]{1,0:T(2,128)} %get-tuple-element.13, f32[2]{0:T(128)S(1)} %get-tuple-element.9), kind=kLoop, calls=%fused_computation.7 | loop fusion | flops 1048576 | bytes 3145736 | tf_op jit(solution)/shard_map/convert_element_type | solution.py:63
  185.6 1.2 copy.80
  (4 shorter events, 0.0 us)
Async XLA Ops:
  7.2 8.8 %copy-start.8 = (bf16[256,640]{1,0:T(8,128)(2,1)S(1)}, bf16[256,640]{1,0:T(8,128)(2,1)}, u32[]{:S(2)}) copy-start(bf16[256,640]{1,0:T(8,128)(2,1)} %param.6) | copy-start | bytes 983044
  7.2 85.3 %all-gather.2.cloned.1.call-start = ((), (), s32[]{:S(2)}) async-start(), calls=%async_computation | async-start | bytes 3145728 | tf_op jit(solution)/shard_map/all_gather | solution.py:73
  7.2 18.3 %collective-permute-start = (bf16[2,256,1024]{2,1,0:T(8,128)(2,1)}, bf16[2,256,1024]{2,1,0:T(8,128)(2,1)S(1)}, u32[]{:S(2)}, u32[]{:S(2)}) collective-permute-start(bf16[2,256,1024]{2,1,0:T(8,128)(2,1)} %param.4), channel_id=1, source_target_pairs={{0,2},{2,4},{4,6},{6,8},{8,10},{10,12},{12,14},{14,16},{16,18},{18... | collective-permute-start | bytes 3145736 | tf_op jit(solution)/shard_map/ppermute | solution.py:14
  7.7 18.7 %collective-permute-start.1 = (bf16[2,256,1024]{2,1,0:T(8,128)(2,1)}, bf16[2,256,1024]{2,1,0:T(8,128)(2,1)}, u32[]{:S(2)}, u32[]{:S(2)}) collective-permute-start(bf16[2,256,1024]{2,1,0:T(8,128)(2,1)} %param.4), channel_id=1, source_target_pairs={{2,0},{4,2},{6,4},{8,6},{10,8},{12,10},{14,12},{16,14},{18,16},{20... | collective-permute-start | bytes 3145736 | tf_op jit(solution)/shard_map/ppermute | solution.py:15
  25.5 1.0 copy-start.7
  34.2 7.3 %copy-start = (bf16[40,2,64,1024]{3,2,1,0:T(8,128)(2,1)S(1)}, bf16[40,2,64,1024]{3,2,1,0:T(8,128)(2,1)}, u32[]{:S(2)}) copy-start(bf16[40,2,64,1024]{3,2,1,0:T(8,128)(2,1)} %gather_fusion) | copy-start | bytes 31457284
  34.2 7.5 %copy-start.6 = (bf16[4,64,10,64]{3,2,1,0:T(8,128)(2,1)S(1)}, bf16[4,64,10,64]{3,2,1,0:T(8,128)(2,1)}, u32[]{:S(2)}) copy-start(bf16[4,64,10,64]{3,2,1,0:T(8,128)(2,1)} %reshape.69) | copy-start | bytes 983044
  84.8 2.3 %copy-start.1 = (f32[2,4,64,1024]{3,2,0,1:T(8,128)S(1)}, f32[2,4,64,1024]{3,2,0,1:T(8,128)}, u32[]{:S(2)}) copy-start(f32[2,4,64,1024]{3,2,0,1:T(8,128)} %get-tuple-element.11) | copy-start | bytes 6291460
  87.3 57.5 %copy-start.9 = (f32[2]{0:T(128)}, f32[2]{0:T(128)S(1)}, u32[]{:S(2)}) copy-start(f32[2]{0:T(128)S(1)} %add_divide_fusion) | copy-start | bytes 28
  92.5 4.7 %copy-start.5 = (f32[1,2,256,1024]{3,1,2,0:T(2,128)S(1)}, f32[1,2,256,1024]{3,1,2,0:T(2,128)}, u32[]{:S(2)}) copy-start(f32[1,2,256,1024]{3,1,2,0:T(2,128)} %copy.56) | copy-start | bytes 6291460
  95.9 1.4 copy-start.4
  97.2 9.2 %copy-start.3 = (bf16[4,256,1024]{2,1,0:T(8,128)(2,1)S(1)}, bf16[4,256,1024]{2,1,0:T(8,128)(2,1)}, u32[]{:S(2)}) copy-start(bf16[4,256,1024]{2,1,0:T(8,128)(2,1)} %all-gather.2.cloned.1.call-done) | copy-start | bytes 6291460
  106.4 3.5 %copy-start.2 = (f32[2,4,64,1024]{3,2,1,0:T(8,128)S(1)}, f32[2,4,64,1024]{3,2,1,0:T(8,128)}, u32[]{:S(2)}) copy-start(f32[2,4,64,1024]{3,2,1,0:T(8,128)} %copy.32) | copy-start | bytes 6291460
Sparse Core Ops, SparseCore 0:
  12.9 32.4 all-gather.1
where the time goes:
time: 194 us
  blocking collectives  98.5 us (51%)
  matrix products  31.6 us (16%)
  local copies, waits for them, and re-layouts  28 us (14%)
  between operations  14.2 us (7%)
  waiting for transfers between devices  7.97 us (4%)
  other arithmetic  7.8 us (4%)
  starting transfers between devices  5.57 us (3%)
    psum x3, blocking collectives, row_reduce(): return lax.psum(values, 'space')  98.5 us
    unnamed x25, local copies, waits for them, and re-layouts  16.4 us
    dot_general x1, matrix products, finish(): jnp.dot(wide_all, flat_r.T, precision=lax.Precision.HIGHEST)  9.15 us
    dot_general x1, matrix products, finish(): jnp.dot(coeffs.T, wide_all, precision=lax.Precision.HIGHEST)  8.71 us
    ppermute x1, waiting for transfers between devices, padded(): before = lax.ppermute(last, axis, up)  7.93 us
    dot_general x1, matrix products, apply_tiles(): jnp.einsum('apbq,kabqw->kapw', h_tiles, picked, preferred_element_type=jn...  6.46 us
    gather x1, local copies, waits for them, and re-layouts, apply_tiles(): picked = blocks[:, links]  5.75 us
    ppermute x1, starting transfers between devices, padded(): after = lax.ppermute(first, axis, down)  5.03 us
  transfers between devices with their start and end apart: 3, of which 1 were waited for; matrix products, arithmetic and copies ran while one was open for 15% of the time, Pallas kernels for 0%

commit v1 on v0

--- a/solution.py
+++ b/solution.py
@@ -37,7 +37,7 @@
     if section == "ritz":
         return lax.psum(values, "space")
     if section == "project":
-        return lax.psum(values, "space")
+        return jnp.sum(lax.all_gather(values, "space"), axis=0)
     return lax.psum(values, "space")
 
 

time: 194 us -> 182 us (0.938)
  blocking collectives: 98.5 us -> 88.3 us
  local copies, waits for them, and re-layouts: 28 us -> 24.2 us
    psum x3 -> x2, blocking collectives: 98.5 us -> 71 us  [row_reduce(): return lax.psum(values, 'space')]
    all_gather x0 -> x1, blocking collectives: none -> 17.4 us  [row_reduce(): return jnp.sum(lax.all_gather(values, 'space'), axis=0)]
    unnamed x25 -> x23, local copies, waits for them, and re-layouts: 16.4 us -> 13.6 us
    dot_general x1, matrix products: 3.51 us -> 5.82 us  [finish(): jnp.dot(flat_all, flat_all.T, preferred_element_type=jnp.float32)]
where the time goes in v1:
time: 182 us
  blocking collectives  88.3 us (49%)
  matrix products  32.4 us (18%)
  local copies, waits for them, and re-layouts  24.2 us (13%)
  between operations  14.2 us (8%)
  other arithmetic  9.43 us (5%)
  waiting for transfers between devices  7.95 us (4%)
  starting transfers between devices  5.57 us (3%)
    psum x2, blocking collectives, row_reduce(): return lax.psum(values, 'space')  71 us
    all_gather x1, blocking collectives, row_reduce(): return jnp.sum(lax.all_gather(values, 'space'), axis=0)  17.4 us
    unnamed x23, local copies, waits for them, and re-layouts  13.6 us
    dot_general x1, matrix products, finish(): jnp.dot(wide_all, flat_r.T, precision=lax.Precision.HIGHEST)  8.94 us
    dot_general x1, matrix products, finish(): jnp.dot(coeffs.T, wide_all, precision=lax.Precision.HIGHEST)  8.66 us
    ppermute x1, waiting for transfers between devices, padded(): before = lax.ppermute(last, axis, up)  7.93 us
    dot_general x1, matrix products, apply_tiles(): jnp.einsum('apbq,kabqw->kapw', h_tiles, picked, preferred_element_type=jn...  6.45 us
    dot_general x1, matrix products, finish(): jnp.dot(flat_all, flat_all.T, preferred_element_type=jnp.float32)  5.82 us
  transfers between devices with their start and end apart: 3, of which 1 were waited for; matrix products, arithmetic and copies ran while one was open for 15% of the time, Pallas kernels for 0%

profile of v1, /device:TPU:0, one launch (start us, length us, event | category | flops | bytes accessed | tf_op | source)
XLA Modules:
  0.0 182.1 jit_solution(441574596630465263)
XLA Ops:
  7.2 0.0 copy-start.7
  7.2 0.0 all-gather.4.cloned.1.call-start
  7.2 0.5 collective-permute-start
  7.7 5.0 %collective-permute-start.1 = (bf16[2,256,1024]{2,1,0:T(8,128)(2,1)}, bf16[2,256,1024]{2,1,0:T(8,128)(2,1)}, u32[]{:S(2)}, u32[]{:S(2)}) collective-permute-start(bf16[2,256,1024]{2,1,0:T(8,128)(2,1)} %param.4), channel_id=1, source_target_pairs={{2,0},{4,2},{6,4},{8,6},{10,8},{12,10},{14,12},{16,14},{18,16},{20... | collective-permute-start | bytes 3145736 | tf_op jit(solution)/shard_map/ppermute | solution.py:15
  12.8 0.0 all-gather.4.cloned.1.call-update
  12.8 0.7 compare_select_fusion
  13.5 0.1 reshape.56
  13.6 2.4 %reshape.74 = bf16[4,64,10,64]{3,2,1,0:T(8,128)(2,1)} reshape(bf16[256,640]{1,0:T(8,128)(2,1)} %param.5) | data formatting | bytes 655360 | tf_op jit(solution)/shard_map/reshape | solution.py:29
  16.0 0.0 copy-done.7
  16.0 1.6 reshape.73
  17.6 7.9 %collective-permute-done = bf16[2,256,1024]{2,1,0:T(8,128)(2,1)S(1)} collective-permute-done((bf16[2,256,1024]{2,1,0:T(8,128)(2,1)}, bf16[2,256,1024]{2,1,0:T(8,128)(2,1)S(1)}, u32[]{:S(2)}, u32[]{:S(2)}) %collective-permute-start) | collective-permute-done | bytes 1048608 | tf_op jit(solution)/shard_map/ppermute | solution.py:14
  25.5 0.0 copy-start.6
  25.5 1.0 copy-done.6
  26.5 0.0 collective-permute-done.1
  26.5 2.0 %pad_maximum_fusion = bf16[2,768,1024]{2,1,0:T(8,128)(2,1)S(1)} fusion(bf16[2,256,1024]{2,1,0:T(8,128)(2,1)} %collective-permute-done.1, bf16[2,256,1024]{2,1,0:T(8,128)(2,1)} %param.4, bf16[2,256,1024]{2,1,0:T(8,128)(2,1)} %copy-done.6), kind=kLoop, calls=%fused_computation.6 | loop fusion | flops 9437184 | bytes 6291456 | tf_op jit(solution)/shard_map/concatenate | solution.py:16
  28.5 5.8 %gather_fusion = bf16[40,2,64,1024]{3,2,1,0:T(8,128)(2,1)} fusion(bf16[2,12,64,1024]{3,2,1,0:T(8,128)(2,1)S(1)} %bitcast.56, s32[1024]{0:T(1024)S(1)} %pad_clamp_fusion), kind=kCustom, calls=%fused_computation | custom fusion | bytes 20971680 | tf_op jit(solution)/shard_map/gather | solution.py:28
  34.2 0.0 copy-start
  34.2 6.5 %fusion.6 = f32[2,4,64,1024]{3,2,0,1:T(8,128)S(1)} fusion(bf16[2,4,10,64,1024]{4,3,0,2,1:T(8,128)(2,1)} %bitcast.57, bf16[4,64,10,64,1]{3,2,1,0,4:T(8,128)(2,1)} %bitcast.70), kind=kOutput, calls=%fused_computation.14 | convolution fusion | flops 671088640 | bytes 12910592 | tf_op jit(solution)/shard_map/apbq,kabqw->kapw/dot_general | solution.py:31
  40.7 0.0 copy-start.5
  40.7 0.2 copy.32
  40.9 0.6 copy-done
  41.5 0.6 copy-done.5
  42.1 2.3 %multiply_reduce_fusion.1 = (f32[2]{0:T(128)S(1)}, f32[2]{0:T(128)S(1)}, f32[2,4,64,1024]{3,2,0,1:T(8,128)S(1)}) fusion(f32[2,4,64,1024]{3,2,0,1:T(8,128)S(1)} %fusion.6, bf16[2,4,10,64,1024]{4,3,0,2,1:T(8,128)(2,1)S(1)} %bitcast.58, bf16[4,64,10,64,1]{3,2,1,0,4:T(8,128)(2,1)S(1)} %bitcast.69), kind=kOutput, calls=%fused_computation.10 | convolution fusion | flops 673185792 | bytes 15007760 | tf_op jit(solution)/shard_map/apbq,kabqw->kapw/dot_general | solution.py:32
  44.4 0.0 copy-start.1
  44.4 0.2 copy.33
  44.6 1.1 copy-done.1
  45.7 2.9 %copy.55 = f32[1,2,256,1024]{3,1,2,0:T(2,128)} copy(f32[1,2,256,1024]{3,2,1,0:T(8,128)S(1)} %bitcast.61) | data formatting | bytes 4194304
  48.6 3.0 %copy.54 = f32[1,2,256,1024]{3,1,2,0:T(2,128)} copy(f32[1,2,256,1024]{3,2,1,0:T(8,128)S(1)} %bitcast.59) | data formatting | bytes 4194304
  51.6 0.0 all-gather.4.cloned.1.call-done
  51.6 5.8 %fusion.12 = f32[4,4]{0,1:T(4,128)S(1)} fusion(bf16[4,256,1024]{2,1,0:T(8,128)(2,1)} %all-gather.4.cloned.1.call-done), kind=kOutput, calls=%fused_computation.16 | convolution fusion | flops 8388608 | bytes 2097216 | tf_op jit(solution)/shard_map/dot_general | solution.py:51
  57.4 39.6 %all-reduce = (f32[2]{0:T(128)S(1)}, f32[2]{0:T(128)S(1)}, f32[4,4]{0,1:T(4,128)S(1)}) all-reduce(f32[2]{0:T(128)S(1)} %get-tuple-element.4, f32[2]{0:T(128)S(1)} %get-tuple-element.3, f32[4,4]{0,1:T(4,128)S(1)} %fusion.12), channel_id=1, replica_groups=mesh['space'=16,'trial'=2] {'space'}, use_global_device_ids=true, to_apply=%region_1.2 | all-reduce | flops 20 | bytes 160 | tf_op jit(solution)/shard_map/psum | solution.py:38
  97.0 0.1 copy.37
  97.1 0.4 cholesky.16
  97.5 0.6 compare_reduce_fusion
  98.2 0.6 fusion.17
  98.8 0.3 custom-call.10
  99.2 0.0 copy-start.8
  99.2 2.1 %multiply_subtract_fusion = f32[2,4,64,1024]{3,2,0,1:T(8,128)S(1)} fusion(f32[2,4,64,1024]{3,2,0,1:T(8,128)S(1)} %fusion.6, f32[2,4,64,1024]{3,2,0,1:T(8,128)} %copy-done.1, f32[2]{0:T(128)S(1)} %add_divide_fusion), kind=kLoop, calls=%fused_computation.9 | loop fusion | flops 1048576 | bytes 6291464 | tf_op jit(solution)/shard_map/sub | solution.py:57
  101.2 0.1 copy.39
  101.4 0.0 copy-start.2
  101.4 1.6 copy.56
  103.0 0.0 copy-done.2
  103.0 1.6 copy.57
  104.7 0.0 copy-start.4
  104.7 0.0 copy-start.3
  104.7 8.9 %convolution_bitcast_fusion = f32[1,4,2]{1,2,0:T(2,128)S(1)} fusion(f32[2,262144]{1,0:T(2,128)S(1)} %bitcast.68, bf16[4,262144]{1,0:T(4,128)(2,1)S(1)} %bitcast.66), kind=kOutput, calls=%fused_computation.17 | convolution fusion | flops 25165824 | bytes 4194336 | tf_op jit(solution)/shard_map/dot_general | solution.py:58
  113.6 0.0 copy-done.4
  113.6 17.4 %all-gather.1 = f32[16,4,2]{1,2,0:T(2,128)S(1)} all-gather(f32[1,4,2]{1,2,0:T(2,128)S(1)} %convolution_bitcast_fusion), channel_id=2, replica_groups=mesh['space'=16,'trial'=2] {'space'}, dimensions={0}, use_global_device_ids=true | all-gather | bytes 544 | tf_op jit(solution)/shard_map/all_gather | solution.py:40
  131.0 0.1 fusion.19
  131.2 0.1 fusion.21
  131.3 0.0 copy-done.8
  131.3 0.0 copy-done.3
  131.3 8.7 %multiply_reduce_fusion = (f32[2]{0:T(128)S(1)}, f32[2,262144]{1,0:T(2,128)}) fusion(f32[4,2]{0,1:T(2,128)S(1)} %fusion.21, bf16[4,262144]{1,0:T(4,128)(2,1)} %bitcast.67, f32[2,262144]{1,0:T(2,128)} %bitcast.65, f32[2,262144]{1,0:T(2,128)S(1)} %bitcast.64, f32[2]{0:T(128)S(1)} %add_divide_fusion), kind=kOutput, calls=%fused_computation.8 | convolution fusion | flops 27787262 | bytes 8388656 | tf_op jit(solution)/shard_map/dot_general | solution.py:60
  140.0 31.4 %psum.31 = f32[2]{0:T(128)S(1)} all-reduce(f32[2]{0:T(128)S(1)} %get-tuple-element.11), channel_id=1, replica_groups=mesh['space'=16,'trial'=2] {'space'}, use_global_device_ids=true, to_apply=%region_9.10 | all-reduce | flops 2 | bytes 16 | tf_op jit(solution)/shard_map/psum | solution.py:41
  171.4 0.5 add_rsqrt_fusion
  171.9 2.1 %multiply_convert_fusion = bf16[2,262144]{1,0:T(2,128)(2,1)S(1)} fusion(f32[2,262144]{1,0:T(2,128)} %get-tuple-element.12, f32[2]{0:T(128)S(1)} %get-tuple-element.8), kind=kLoop, calls=%fused_computation.7 | loop fusion | flops 1048576 | bytes 3145736 | tf_op jit(solution)/shard_map/convert_element_type | solution.py:63
  174.0 1.2 copy.80
  (5 shorter events, 0.1 us)
Async XLA Ops:
  7.2 8.8 %copy-start.7 = (bf16[256,640]{1,0:T(8,128)(2,1)S(1)}, bf16[256,640]{1,0:T(8,128)(2,1)}, u32[]{:S(2)}) copy-start(bf16[256,640]{1,0:T(8,128)(2,1)} %param.6) | copy-start | bytes 983044
  7.2 44.4 %all-gather.4.cloned.1.call-start = ((), (), s32[]{:S(2)}) async-start(), calls=%async_computation | async-start | bytes 3145728 | tf_op jit(solution)/shard_map/all_gather | solution.py:73
  7.2 18.3 %collective-permute-start = (bf16[2,256,1024]{2,1,0:T(8,128)(2,1)}, bf16[2,256,1024]{2,1,0:T(8,128)(2,1)S(1)}, u32[]{:S(2)}, u32[]{:S(2)}) collective-permute-start(bf16[2,256,1024]{2,1,0:T(8,128)(2,1)} %param.4), channel_id=1, source_target_pairs={{0,2},{2,4},{4,6},{6,8},{8,10},{10,12},{12,14},{14,16},{16,18},{18... | collective-permute-start | bytes 3145736 | tf_op jit(solution)/shard_map/ppermute | solution.py:14
  7.7 18.7 %collective-permute-start.1 = (bf16[2,256,1024]{2,1,0:T(8,128)(2,1)}, bf16[2,256,1024]{2,1,0:T(8,128)(2,1)}, u32[]{:S(2)}, u32[]{:S(2)}) collective-permute-start(bf16[2,256,1024]{2,1,0:T(8,128)(2,1)} %param.4), channel_id=1, source_target_pairs={{2,0},{4,2},{6,4},{8,6},{10,8},{12,10},{14,12},{16,14},{18,16},{20... | collective-permute-start | bytes 3145736 | tf_op jit(solution)/shard_map/ppermute | solution.py:15
  25.5 1.0 copy-start.6
  34.2 7.3 %copy-start = (bf16[40,2,64,1024]{3,2,1,0:T(8,128)(2,1)S(1)}, bf16[40,2,64,1024]{3,2,1,0:T(8,128)(2,1)}, u32[]{:S(2)}) copy-start(bf16[40,2,64,1024]{3,2,1,0:T(8,128)(2,1)} %gather_fusion) | copy-start | bytes 31457284
  40.7 1.4 copy-start.5
  44.4 1.3 copy-start.1
  99.2 32.1 %copy-start.8 = (f32[2]{0:T(128)}, f32[2]{0:T(128)S(1)}, u32[]{:S(2)}) copy-start(f32[2]{0:T(128)S(1)} %add_divide_fusion) | copy-start | bytes 28
  101.4 1.6 copy-start.2
  104.7 9.0 %copy-start.4 = (bf16[1,4,256,1024]{3,1,2,0:T(4,128)(2,1)}, bf16[1,4,256,1024]{3,1,2,0:T(4,128)(2,1)S(1)}, u32[]{:S(2)}) copy-start(bf16[1,4,256,1024]{3,1,2,0:T(4,128)(2,1)S(1)} %copy.57) | copy-start | bytes 6291460
  104.7 26.6 %copy-start.3 = (f32[1,2,256,1024]{3,1,2,0:T(2,128)S(1)}, f32[1,2,256,1024]{3,1,2,0:T(2,128)}, u32[]{:S(2)}) copy-start(f32[1,2,256,1024]{3,1,2,0:T(2,128)} %copy.55) | copy-start | bytes 6291460
Sparse Core Ops, SparseCore 0:
  12.9 32.4 all-gather.3
